TPU v7x, 32 devices: a whole 2x2x4 slice. The times are simulated.
32 devices in a mesh: groups: 2 (over x), seq: 16 (over z, y, core).
Axes of the slice: x: 2, y: 2, z: 4, core: 2. Of those that a mesh axis runs over, the one named last changes fastest.
Arguments:
- queries: bfloat16 [4096, 2048], P(('groups', 'seq')), parts along dimension 0, may hold values from -140 to 140
- keys: bfloat16 [4096, 2048], P(('groups', 'seq')), parts along dimension 0, may hold values from -6.25 to 6.25
- values: bfloat16 [4096, 2048], P(('groups', 'seq')), parts along dimension 0, may hold values from -6 to 6
- grad_out: bfloat16 [4096, 2048], P(('groups', 'seq')), parts along dimension 0, may hold values from -6 to 6
- partners: int32 [32, 16, 3], P(('groups', 'seq')), parts along dimension 0, may hold values from 0 to 15, all different within a row; in each aligned block of 16 rows (0 to 15, 16 to 31, ..., all dimensions but the last counted through in order) at most 3 rows name the same one
Outputs:
- grad_queries: bfloat16 [4096, 2048], P(('groups', 'seq')), parts along dimension 0
- grad_keys: bfloat16 [4096, 2048], P(('groups', 'seq')), parts along dimension 0
- grad_values: bfloat16 [4096, 2048], P(('groups', 'seq')), parts along dimension 0
There are 2 independent parts, one for each index of `groups`. A program takes and returns all parts, laid end to end along the dimension named above; each array names one. Nothing has to cross between parts.
Inputs may be any that keep to these rules, and one draw needn't show every extreme that they name: In the 16 head rows of one query block, no block is named more than 3 times, and some block is named exactly 3 times; the 3 partners of one head are different blocks.
All inputs are finite; a program needn't handle non-finite values.
Results may differ from a plain program's by a relative error of at most 0.01.
Values may be sent and summed in bfloat16 or wider, within the bound.
A program may use at most 128 MiB of HBM per device.

v0:
```python
import math
import jax
import jax.numpy as jnp
from jax import lax
from jax.sharding import PartitionSpec as P

H = 16
HD = 128


def with_halo(shard, sides, width):
    for axis, dim in sides:
        count, length = (lax.axis_size(axis), shard.shape[dim])
        up = [(i, (i + 1) % count) for i in range(count - 1)]
        down = [(j, i) for i, j in up]
        last = lax.slice_in_dim(shard, length - width, length, axis=dim)
        first = lax.slice_in_dim(shard, 0, width, axis=dim)
        before = lax.ppermute(last, axis, up)
        after = lax.ppermute(first, axis, down)
        shard = jnp.concatenate([before, shard, after], axis=dim)
    return shard


def broadcast(block, axis, source):
    block = jnp.where(lax.axis_index(axis) == source, block, jnp.zeros_like(block))
    return lax.psum(block, axis)


def per_device(queries, keys, values, grad_out, partners):
    devices = lax.axis_size("seq")
    my_index = lax.axis_index("seq")
    most_slots = max(2, (3 * H + devices - 1) // devices)
    softmax_scale = 1.0 / math.sqrt(HD)
    width = H * HD
    rows_here = queries.shape[0]
    kv_local = jnp.stack([keys, values])
    query_heads = queries.reshape(rows_here, H, HD)
    grad_heads = grad_out.reshape(rows_here, H, HD)
    lower_ok = my_index > 0
    upper_ok = my_index < devices - 1
    window = with_halo(kv_local, (("seq", 1),), rows_here)
    sink_parts = [broadcast(kv_local, "seq", sink_root) for sink_root in range(2)]
    near_kv = jnp.concatenate([window] + sink_parts, axis=1).reshape(2, 5 * rows_here, H, HD)
    near_keys = near_kv[0]
    near_values = near_kv[1]
    item_count = 3 * H
    dests = partners.reshape(item_count)
    item_heads = jnp.arange(item_count, dtype=jnp.int32) // 3
    dest_hot = (dests[:, None] == jnp.arange(devices, dtype=jnp.int32)[None, :]).astype(jnp.int32)
    slot_rank = jnp.sum((jnp.cumsum(dest_hot, axis=0) - dest_hot) * dest_hot, axis=1)
    kv_by_head = kv_local.reshape(2, rows_here, H, HD).transpose(2, 0, 1, 3)
    requests = jnp.full((devices, most_slots), -1, jnp.int32).at[dests, slot_rank].set(item_heads)
    wanted = lax.all_to_all(requests, "seq", split_axis=0, concat_axis=0, tiled=True)
    picked = kv_by_head[jnp.maximum(wanted, 0)]
    fetched = lax.all_to_all(
        jnp.where((wanted >= 0)[:, :, None, None, None], picked, jnp.zeros_like(picked)),
        "seq",
        split_axis=0,
        concat_axis=0,
        tiled=True,
    )
    far_kv = fetched[dests, slot_rank].reshape(H, 3, 2, rows_here, HD)
    far_keys = far_kv[:, :, 0]
    far_values = far_kv[:, :, 1]
    near_scores = softmax_scale * jnp.einsum(
        "thd,khd->htk", query_heads, near_keys, preferred_element_type=jnp.float32
    )
    far_scores = softmax_scale * jnp.einsum(
        "thd,hrkd->htrk", query_heads, far_keys, preferred_element_type=jnp.float32
    )
    key_pos = jnp.arange(5 * rows_here, dtype=jnp.int32)
    key_ok = jnp.logical_not((key_pos < rows_here) & jnp.logical_not(lower_ok))
    key_ok = key_ok & jnp.logical_not(
        (key_pos >= 2 * rows_here) & (key_pos < 3 * rows_here) & jnp.logical_not(upper_ok)
    )
    near_max = jnp.max(
        jnp.where(key_ok[None, None, :], near_scores, -jnp.inf), axis=2, keepdims=True
    )
    far_max = jnp.max(far_scores, axis=(2, 3))[:, :, None]
    row_max = jnp.maximum(near_max, far_max)
    near_total = jnp.sum(
        jnp.where(key_ok[None, None, :], jnp.exp(near_scores - row_max), 0.0), axis=2, keepdims=True
    )
    far_total = jnp.sum(jnp.exp(far_scores - row_max[:, :, :, None]), axis=(2, 3))[:, :, None]
    totals = near_total + far_total

    def near_prob_f32():
        return jnp.where(key_ok[None, None, :], jnp.exp(near_scores - row_max), 0.0) / totals

    def far_prob_f32():
        return jnp.exp(far_scores - row_max[:, :, :, None]) / totals[:, :, :, None]

    near_probs = near_prob_f32().astype(jnp.bfloat16)
    far_probs = far_prob_f32().astype(jnp.bfloat16)
    attended = jnp.einsum(
        "htk,khd->htd", near_probs, near_values, preferred_element_type=jnp.float32
    )
    attended = attended + jnp.einsum(
        "htrk,hrkd->htd", far_probs, far_values, preferred_element_type=jnp.float32
    )
    delta = jnp.sum(grad_heads.transpose(1, 0, 2) * attended, axis=2)
    near_dprob = jnp.einsum(
        "thd,khd->htk", grad_heads, near_values, preferred_element_type=jnp.float32
    )
    far_dprob = jnp.einsum(
        "thd,hrkd->htrk", grad_heads, far_values, preferred_element_type=jnp.float32
    )
    near_dscore = (near_prob_f32() * (near_dprob - delta[:, :, None])).astype(jnp.bfloat16)
    far_dscore = (far_prob_f32() * (far_dprob - delta[:, :, None, None])).astype(jnp.bfloat16)
    grad_q = jnp.einsum("htk,khd->thd", near_dscore, near_keys, preferred_element_type=jnp.float32)
    grad_q = grad_q + jnp.einsum(
        "htrk,hrkd->thd", far_dscore, far_keys, preferred_element_type=jnp.float32
    )
    grad_queries = (softmax_scale * grad_q).reshape(rows_here, width).astype(jnp.bfloat16)
    near_key_term = softmax_scale * jnp.einsum(
        "htk,thd->khd", near_dscore, query_heads, preferred_element_type=jnp.float32
    )
    near_value_term = jnp.einsum(
        "htk,thd->khd", near_probs, grad_heads, preferred_element_type=jnp.float32
    )
    near_terms = jnp.stack(
        [near_key_term.reshape(5 * rows_here, width), near_value_term.reshape(5 * rows_here, width)]
    )
    own_grads = near_terms[:, rows_here : 2 * rows_here]
    outgoing = jnp.concatenate(
        [near_terms[:, :rows_here], near_terms[:, 2 * rows_here : 3 * rows_here]], axis=1
    )
    incoming = with_halo(outgoing.astype(jnp.bfloat16), (("seq", 1),), rows_here).astype(
        outgoing.dtype
    )
    own_grads = own_grads + incoming[:, :rows_here] + incoming[:, 3 * rows_here :]
    sink_terms = (
        near_terms[:, 3 * rows_here :].reshape(2, 2, rows_here, width).transpose(1, 0, 2, 3)
    )
    sink_total = lax.psum(sink_terms, "seq")
    sink_mine = lax.dynamic_index_in_dim(sink_total, jnp.minimum(my_index, 1), 0, keepdims=False)
    own_grads = own_grads + jnp.where(my_index < 2, sink_mine, jnp.zeros_like(sink_mine))
    far_key_term = softmax_scale * jnp.einsum(
        "htrk,thd->hrkd", far_dscore, query_heads, preferred_element_type=jnp.float32
    )
    far_value_term = jnp.einsum(
        "htrk,thd->hrkd", far_probs, grad_heads, preferred_element_type=jnp.float32
    )
    far_terms = (
        jnp.stack([far_key_term, far_value_term], axis=2)
        .astype(jnp.bfloat16)
        .reshape(item_count, 2, rows_here, HD)
    )
    outbox = (
        jnp.zeros((devices, most_slots, 2, rows_here, HD), jnp.bfloat16)
        .at[dests, slot_rank]
        .set(far_terms)
    )
    returned = lax.all_to_all(outbox, "seq", split_axis=0, concat_axis=0, tiled=True)
    head_hot = (wanted[:, :, None] == jnp.arange(H, dtype=jnp.int32)[None, None, :]).astype(
        jnp.bfloat16
    )
    gained = jnp.einsum("nmh,nmcbd->cbhd", head_hot, returned, preferred_element_type=jnp.float32)
    own_grads = own_grads + gained.reshape(2, rows_here, width)
    return (grad_queries, own_grads[0].astype(jnp.bfloat16), own_grads[1].astype(jnp.bfloat16))


def solution(mesh):
    placed = (
        P(("groups", "seq"), None),
        P(("groups", "seq"), None),
        P(("groups", "seq"), None),
        P(("groups", "seq"), None),
        P(("groups", "seq"), None, None),
    )
    return jax.shard_map(
        per_device,
        mesh=mesh,
        in_specs=placed,
        out_specs=(
            P(("groups", "seq"), None),
            P(("groups", "seq"), None),
            P(("groups", "seq"), None),
        ),
        check_vma=False,
    )
```

profile of v0, /device:TPU:0, one launch (start us, length us, event | category | flops | bytes accessed | tf_op | source)
XLA Modules:
  0.0 459.0 jit_solution(7758403241742781614)
XLA Ops:
  8.5 2.8 scatter_fusion
  12.0 7.4 %all-to-all-start = ((s32[16,1,3]{2,1,0:T(1,128)}), s32[16,1,3]{2,1,0:T(1,128)S(1)}, u32[]{:S(2)}, u32[]{:S(2)}) async-start(s32[16,1,3]{2,1,0:T(1,128)} %copy.159), calls=%async_computation | async-start | bytes 16384 | tf_op jit(solution)/shard_map/all_to_all | solution.py:53
  21.7 4.0 all-to-all-done
  26.0 2.7 gather_fusion
  28.7 3.8 broadcast_select_fusion
  32.5 4.5 all-to-all-start.1
  48.5 2.4 constant_dynamic-update-slice_fusion.2
  50.9 169.4 %all-reduce.6.cloned.1.call-done = (bf16[2,128,2048]{1,2,0:T(8,128)(2,1)}, bf16[2,128,2048]{1,2,0:T(8,128)(2,1)}) async-done(((bf16[2,128,2048]{1,2,0:T(8,128)(2,1)}, bf16[2,128,2048]{1,2,0:T(8,128)(2,1)}), (bf16[2,128,2048]{1,2,0:T(8,128)(2,1)}, bf16[2,128,2048]{1,2,0:T(8,128)(2,1)})) %all-reduce.6.cloned.1.call-update) | async-done | bytes 2097168 | tf_op jit(solution)/shard_map/psum | solution.py:26
  220.3 2.4 constant_dynamic-update-slice_fusion.1
  222.7 2.3 constant_dynamic-update-slice_fusion
  225.0 4.6 %fusion.52 = (bf16[1,640,2048]{1,2,0:T(8,128)(2,1)}, bf16[1,640,2048]{1,2,0:T(8,128)(2,1)S(1)}) fusion(bf16[2,640,2048]{1,2,0:T(8,128)(2,1)} %constant_dynamic-update-slice_fusion), kind=kLoop, calls=%fused_computation.102 | loop fusion | bytes 10485760 | tf_op jit(solution)/shard_map/slice | solution.py:45
  229.6 3.7 select_reduce_fusion
  233.3 4.7 %gather_fusion.1 = bf16[48,2,128,128]{3,2,1,0:T(8,128)(2,1)} fusion(bf16[16,3,2,128,128]{4,3,2,1,0:T(8,128)(2,1)} %all-to-all-done.1, s32[48]{0:T(128)S(1)} %bitcast.171), kind=kCustom, calls=%fused_computation.1 | custom fusion | bytes 6291840 | tf_op jit(solution)/shard_map/gather | solution.py:62
  240.7 3.0 copy-done.2
  254.3 2.5 broadcast.125
  256.9 9.6 %scatter_fusion.1 = bf16[16,3,2,128,128]{4,3,2,1,0:T(8,128)(2,1)} fusion(bf16[16,3,2,128,128]{4,3,2,1,0:T(8,128)(2,1)} %broadcast.125, s32[48]{0:T(128)S(1)} %get-tuple-element.20, bf16[48,2,128,128]{3,2,1,0:T(8,128)(2,1)} %pad_maximum_fusion.1), kind=kCustom, calls=%fused_computation.3 | custom fusion | bytes 9437568 | tf_op jit(solution)/shard_map/scatter | solution.py:152
  266.4 4.5 all-to-all-start.2
  271.0 5.7 %fusion.1 = bf16[16,128,640]{1,2,0:T(8,128)(2,1)S(1)} fusion(f32[16,128]{1,0:T(8,128)S(1)} %fusion.29, bf16[640,16,128]{0,2,1:T(8,128)(2,1)} %bitcast.167, bf16[128,16,128]{0,2,1:T(8,128)(2,1)} %bitcast.173, f32[16,128]{1,0:T(8,128)S(1)} %add.70, f32[16,128]{1,0:T(8,128)S(1)} %max.27, f32[16,640,128]{2,1,0:T(8,128)} %get-tuple-element.32, ...), kind=kOutput, calls=%fused_computation.11 | convolution fusion | flops 344719360 | bytes 11035264 | tf_op jit(solution)/shard_map/thd,khd->htk/dot_general | solution.py:102
  278.3 3.2 multiply_bitcast_fusion
  281.5 6.0 %copy.181 = f32[640,16,128]{0,2,1:T(8,128)} copy(f32[640,16,128]{2,0,1:T(8,128)} %multiply_bitcast_fusion) | data formatting | bytes 10485760 | tf_op jit(solution)/shard_map/mul | solution.py:115
  287.4 4.1 fusion.25
  291.6 2.3 copy-done.1
  293.9 2.3 fusion.2
  296.2 5.4 %copy.183 = f32[2,256,2048]{2,1,0:T(8,128)} copy(f32[2,256,2048]{1,2,0:T(8,128)} %fusion.2) | data formatting | bytes 8388608 | tf_op jit(solution)/shard_map/slice | solution.py:133
  301.6 5.3 %copy.184 = f32[2,2,128,2048]{2,3,0,1:T(8,128)} copy(f32[2,2,128,2048]{3,2,1,0:T(8,128)} %bitcast.151) | data formatting | bytes 8388608 | tf_op jit(solution)/shard_map/reshape | solution.py:133
  307.0 4.8 %fusion = bf16[2,640,2048]{1,2,0:T(8,128)(2,1)S(1)} fusion(f32[1,640,2048]{1,2,0:T(8,128)} %bitcast.146, f32[1,640,2048]{1,2,0:T(8,128)} %bitcast.142), kind=kLoop, calls=%fused_computation.9 | loop fusion | flops 2621440 | bytes 15728640 | tf_op jit(solution)/shard_map/convert.9
  314.7 4.0 collective-permute-start.2
  318.7 2.8 fusion.22
  323.4 14.6 %all-to-all-done.2 = bf16[16,3,2,128,128]{4,3,2,1,0:T(8,128)(2,1)} async-done(((bf16[16,3,2,128,128]{4,3,2,1,0:T(8,128)(2,1)}), bf16[16,3,2,128,128]{4,3,2,1,0:T(8,128)(2,1)}, u32[]{:S(2)}, u32[]{:S(2)}) %all-to-all-start.2) | async-done | bytes 3145760 | tf_op jit(solution)/shard_map/all_to_all | solution.py:154
  338.0 5.0 %fusion.15 = f32[2,128,16,128]{3,2,1,0:T(8,128)} fusion(bf16[16,3,2,128,128]{4,3,2,1,0:T(8,128)(2,1)} %all-to-all-done.2, s32[16,3]{0,1:T(4,128)S(1)} %bitcast.178), kind=kOutput, calls=%fused_computation.37 | convolution fusion | flops 50332416 | bytes 5243072 | tf_op jit(solution)/shard_map/nmh,nmcbd->cbhd/dot_general | solution.py:158
  345.1 101.8 %all-reduce.4.cloned.1.call-done = f32[2,2,128,2048]{2,3,1,0:T(8,128)} async-done(((f32[2,2,128,2048]{2,3,1,0:T(8,128)}), f32[2,2,128,2048]{2,3,1,0:T(8,128)}) %all-reduce.4.cloned.1.call-update) | async-done | bytes 4194320 | tf_op jit(solution)/shard_map/psum | solution.py:135
  446.9 3.2 fusion.14
  (89 shorter events, 39.9 us)
Async XLA Ops:
  7.2 13.8 %copy-start.11 = (bf16[128,2048]{1,0:T(8,128)(2,1)S(1)}, bf16[128,2048]{1,0:T(8,128)(2,1)}, u32[]{:S(2)}) copy-start(bf16[128,2048]{1,0:T(8,128)(2,1)} %param.6) | copy-start | bytes 1572868
  12.0 13.7 %all-to-all-start = ((s32[16,1,3]{2,1,0:T(1,128)}), s32[16,1,3]{2,1,0:T(1,128)S(1)}, u32[]{:S(2)}, u32[]{:S(2)}) async-start(s32[16,1,3]{2,1,0:T(1,128)} %copy.159), calls=%async_computation | async-start | bytes 16384 | tf_op jit(solution)/shard_map/all_to_all | solution.py:53
  32.5 200.8 %all-to-all-start.1 = ((bf16[16,3,2,128,128]{4,3,2,1,0:T(8,128)(2,1)}), bf16[16,3,2,128,128]{4,3,2,1,0:T(8,128)(2,1)}, u32[]{:S(2)}, u32[]{:S(2)}) async-start(bf16[16,3,2,128,128]{4,3,2,1,0:T(8,128)(2,1)} %broadcast_select_fusion), calls=%async_computation.1 | async-start | bytes 6291456 | tf_op jit(solution)/shard_map/all_to_all | solution.py:55
  37.0 183.3 %all-reduce.6.cloned.1.call-start = ((), (), s32[]{:S(2)}) async-start(), calls=%async_computation.4 | async-start | bytes 4194304 | tf_op jit(solution)/shard_map/psum | solution.py:26
  37.2 4.4 collective-permute-start
  39.4 9.1 %collective-permute-start.1 = (bf16[2,128,2048]{1,2,0:T(8,128)(2,1)S(1)}, bf16[2,128,2048]{1,2,0:T(8,128)(2,1)}, u32[]{:S(2)}, u32[]{:S(2)}) collective-permute-start(bf16[2,128,2048]{1,2,0:T(8,128)(2,1)S(1)} %pad_maximum_fusion.5), channel_id=1, source_target_pairs={{1,0},{2,1},{3,2},{4,3},{5,4},{6,5},{7,6},{8,7},{9,8},{10,9},{11,1... | collective-permute-start | bytes 3145736 | tf_op jit(solution)/shard_map/ppermute | solution.py:19
  41.8 4.3 copy-start.12
  43.8 2.3 copy-start.6
  46.1 1.0 copy-start.13
  225.0 4.6 %copy-start.8 = (bf16[128,16,128]{0,2,1:T(8,128)(2,1)S(1)}, bf16[128,16,128]{0,2,1:T(8,128)(2,1)}, u32[]{:S(2)}) copy-start(bf16[128,16,128]{0,2,1:T(8,128)(2,1)} %copy.179) | copy-start | bytes 1572868
  240.1 10.0 %copy-start.3 = (bf16[48,2,128,128]{3,2,0,1:T(8,128)(2,1)}, bf16[48,2,128,128]{3,2,0,1:T(8,128)(2,1)S(1)}, u32[]{:S(2)}) copy-start(bf16[48,2,128,128]{3,2,0,1:T(8,128)(2,1)S(1)} %copy.166) | copy-start | bytes 9437188
  240.1 3.6 copy-start.2
  245.4 1.1 copy-start.14
  246.5 1.7 copy-start.10
  251.0 1.1 copy-start.7
  266.4 71.6 %all-to-all-start.2 = ((bf16[16,3,2,128,128]{4,3,2,1,0:T(8,128)(2,1)}), bf16[16,3,2,128,128]{4,3,2,1,0:T(8,128)(2,1)}, u32[]{:S(2)}, u32[]{:S(2)}) async-start(bf16[16,3,2,128,128]{4,3,2,1,0:T(8,128)(2,1)} %scatter_fusion.1), calls=%async_computation.2 | async-start | bytes 6291456 | tf_op jit(solution)/shard_map/all_to_all | solution.py:154
  270.9 7.4 %copy-start.9 = (bf16[128,16,128]{0,2,1:T(8,128)(2,1)S(1)}, bf16[128,16,128]{0,2,1:T(8,128)(2,1)}, u32[]{:S(2)}) copy-start(bf16[128,16,128]{0,2,1:T(8,128)(2,1)} %copy.179) | copy-start | bytes 1572868
  270.9 175.9 %all-reduce.4.cloned.1.call-start = ((), (), s32[]{:S(2)}) async-start(), calls=%async_computation.3 | async-start | bytes 8388608 | tf_op jit(solution)/shard_map/psum | solution.py:135
  276.7 1.6 copy-start.4
  281.5 6.0 %copy-start.15 = (bf16[128,2048]{0,1:T(8,128)(2,1)S(1)}, bf16[128,2048]{0,1:T(8,128)(2,1)}, u32[]{:S(2)}) copy-start(bf16[128,2048]{0,1:T(8,128)(2,1)} %copy.168) | copy-start | bytes 1572868
  287.4 6.5 %copy-start = (f32[640,16,128]{0,2,1:T(8,128)S(1)}, f32[640,16,128]{0,2,1:T(8,128)}, u32[]{:S(2)}) copy-start(f32[640,16,128]{0,2,1:T(8,128)} %copy.181) | copy-start | bytes 15728644
  291.6 2.3 copy-start.1
  313.4 31.7 %collective-permute-start.3 = (bf16[2,128,2048]{1,2,0:T(8,128)(2,1)}, bf16[2,128,2048]{1,2,0:T(8,128)(2,1)}, u32[]{:S(2)}, u32[]{:S(2)}) collective-permute-start(bf16[2,128,2048]{1,2,0:T(8,128)(2,1)} %get-tuple-element.23), channel_id=1, source_target_pairs={{1,0},{2,1},{3,2},{4,3},{5,4},{6,5},{7,6},{8,7},{9,8},{10,9},{11,1... | collective-permute-start | bytes 3145736 | tf_op jit(solution)/shard_map/ppermute | solution.py:19
  314.7 30.4 %collective-permute-start.2 = (bf16[2,128,2048]{1,2,0:T(8,128)(2,1)}, bf16[2,128,2048]{1,2,0:T(8,128)(2,1)}, u32[]{:S(2)}, u32[]{:S(2)}) collective-permute-start(bf16[2,128,2048]{1,2,0:T(8,128)(2,1)} %get-tuple-element.22), channel_id=1, source_target_pairs={{0,1},{1,2},{2,3},{3,4},{4,5},{5,6},{6,7},{7,8},{8,9},{9,10},{10,1... | collective-permute-start | bytes 3145736 | tf_op jit(solution)/shard_map/ppermute | solution.py:18
  318.7 2.8 copy-start.5
Sparse Core Ops, SparseCore 0:
  46.2 173.9 all-reduce.5
  307.1 139.7 all-reduce.3
where the time goes:
time: 460 us; the launch traced here: 459 us
  waiting for transfers between devices  291 us (63%)
  local copies, waits for them, and re-layouts  76.9 us (17%)
  matrix products  31.2 us (7%)
  starting transfers between devices  25.4 us (6%)
  other arithmetic  20.4 us (4%)
  between operations  14.5 us (3%)
    psum x1, waiting for transfers between devices, broadcast(): return lax.psum(block, axis)  169 us
    psum x1, waiting for transfers between devices, per_device(): sink_total = lax.psum(sink_terms, 'seq')  102 us
    unnamed x43, local copies, waits for them, and re-layouts  22.3 us
    all_to_all x1, waiting for transfers between devices, per_device(): lax.all_to_all(outbox, 'seq', split_axis=0, concat_axis=0, tiled=True)  14.6 us
    scatter x1, local copies, waits for them, and re-layouts, per_device(): outbox = jnp.zeros((devices, most_slots, 2, rows_here, HD), jnp.bfloat16)...  9.56 us
  transfers between devices with their start and end apart: 9, of which 5 were waited for; matrix products, arithmetic and copies ran while one was open for 16% of the time, Pallas kernels for 0%

commit v1 on v0

--- a/solution.py
+++ b/solution.py
@@ -6,6 +6,22 @@
 
 H = 16
 HD = 128
+
+
+def pairwise_exchange(x, axis, split, join):
+    ways, here = (lax.axis_size(axis), lax.axis_index(axis))
+    width = x.shape[split] // ways
+    dims = list(x.shape)
+    dims[split] = width
+    height = dims[join]
+    dims[join] = height * ways
+    full = jnp.zeros(dims, x.dtype)
+    for mask in range(ways):
+        part = lax.dynamic_slice_in_dim(x, (here ^ mask) * width, width, axis=split)
+        if mask:
+            part = lax.ppermute(part, axis, [(d, d ^ mask) for d in range(ways)])
+        full = lax.dynamic_update_slice_in_dim(full, part, (here ^ mask) * height, axis=join)
+    return full
 
 
 def with_halo(shard, sides, width):
@@ -50,7 +66,7 @@
     slot_rank = jnp.sum((jnp.cumsum(dest_hot, axis=0) - dest_hot) * dest_hot, axis=1)
     kv_by_head = kv_local.reshape(2, rows_here, H, HD).transpose(2, 0, 1, 3)
     requests = jnp.full((devices, most_slots), -1, jnp.int32).at[dests, slot_rank].set(item_heads)
-    wanted = lax.all_to_all(requests, "seq", split_axis=0, concat_axis=0, tiled=True)
+    wanted = pairwise_exchange(requests, "seq", 0, 0)
     picked = kv_by_head[jnp.maximum(wanted, 0)]
     fetched = lax.all_to_all(
         jnp.where((wanted >= 0)[:, :, None, None, None], picked, jnp.zeros_like(picked)),

time: 460 us -> 478 us (1.039)
  starting transfers between devices: 25.4 us -> 40.7 us
    ppermute x0 -> x15, starting transfers between devices: none -> 22.7 us  [pairwise_exchange(): part = lax.ppermute(part, axis, [(d, d ^ mask) for d in range(ways)])]
    all_to_all x1 -> x0, starting transfers between devices: 7.39 us -> none  [per_device(): lax.all_to_all(requests, 'seq', split_axis=0, concat_axis=0, tiled=True)]
    ppermute x0 -> x15, waiting for transfers between devices: none -> 5.07 us  [pairwise_exchange(): part = lax.ppermute(part, axis, [(d, d ^ mask) for d in range(ways)])]
  transfers between devices with their start and end apart: 9 -> 23, of which waited for: 5 -> 6; matrix products, arithmetic and copies ran while one was open for 16% -> 16% of each run, Pallas kernels for 0% -> 0%
where the time goes in v1:
time: 478 us; the launch traced here: 477 us
  waiting for transfers between devices  291 us (61%)
  local copies, waits for them, and re-layouts  78.4 us (16%)
  starting transfers between devices  40.7 us (9%)
  matrix products  31.1 us (7%)
  other arithmetic  20.4 us (4%)
  between operations  14.7 us (3%)
    psum x1, waiting for transfers between devices, broadcast(): return lax.psum(block, axis)  169 us
    psum x1, waiting for transfers between devices, per_device(): sink_total = lax.psum(sink_terms, 'seq')  102 us
    ppermute x15, starting transfers between devices, pairwise_exchange(): part = lax.ppermute(part, axis, [(d, d ^ mask) for d in range(ways)])  22.7 us
    unnamed x43, local copies, waits for them, and re-layouts  22.4 us
    all_to_all x1, waiting for transfers between devices, per_device(): lax.all_to_all(outbox, 'seq', split_axis=0, concat_axis=0, tiled=True)  14.4 us
    scatter x1, local copies, waits for them, and re-layouts, per_device(): outbox = jnp.zeros((devices, most_slots, 2, rows_here, HD), jnp.bfloat16)...  9.68 us
  transfers between devices with their start and end apart: 23, of which 6 were waited for; matrix products, arithmetic and copies ran while one was open for 16% of the time, Pallas kernels for 0%

profile of v1, /device:TPU:0, one launch (start us, length us, event | category | flops | bytes accessed | tf_op | source)
XLA Modules:
  0.0 476.6 jit_solution(15811468159235494592)
XLA Ops:
  8.7 2.8 scatter_fusion
  12.1 2.6 collective-permute-start.3
  19.0 2.7 collective-permute-start.7
  22.1 2.7 collective-permute-start.9
  25.1 3.6 collective-permute-start.11
  29.1 3.6 collective-permute-start.13
  33.1 4.5 collective-permute-start.15
  39.5 3.9 collective-permute-done.16
  43.7 2.7 gather_fusion
  46.4 3.8 broadcast_select_fusion
  50.2 4.5 all-to-all-start
  68.6 169.4 %all-reduce.6.cloned.1.call-done = (bf16[2,128,2048]{1,2,0:T(8,128)(2,1)}, bf16[2,128,2048]{1,2,0:T(8,128)(2,1)}) async-done(((bf16[2,128,2048]{1,2,0:T(8,128)(2,1)}, bf16[2,128,2048]{1,2,0:T(8,128)(2,1)}), (bf16[2,128,2048]{1,2,0:T(8,128)(2,1)}, bf16[2,128,2048]{1,2,0:T(8,128)(2,1)})) %all-reduce.6.cloned.1.call-update) | async-done | bytes 2097168 | tf_op jit(solution)/shard_map/psum | solution.py:42
  242.7 4.6 fusion.52
  247.3 3.7 select_reduce_fusion
  251.0 4.6 gather_fusion.1
  258.4 3.0 copy-done.2
  272.0 2.5 broadcast.111
  274.4 9.7 %scatter_fusion.1 = bf16[16,3,2,128,128]{4,3,2,1,0:T(8,128)(2,1)} fusion(bf16[16,3,2,128,128]{4,3,2,1,0:T(8,128)(2,1)} %broadcast.111, s32[48]{0:T(128)S(1)} %get-tuple-element.20, bf16[48,2,128,128]{3,2,1,0:T(8,128)(2,1)} %pad_maximum_fusion.1), kind=kCustom, calls=%fused_computation.3 | custom fusion | bytes 9437568 | tf_op jit(solution)/shard_map/scatter | solution.py:168
  284.1 4.5 all-to-all-start.1
  288.7 5.7 %fusion.1 = bf16[16,128,640]{1,2,0:T(8,128)(2,1)S(1)} fusion(f32[16,128]{1,0:T(8,128)S(1)} %fusion.29, bf16[640,16,128]{0,2,1:T(8,128)(2,1)} %bitcast.163, bf16[128,16,128]{0,2,1:T(8,128)(2,1)} %bitcast.169, f32[16,128]{1,0:T(8,128)S(1)} %add.150, f32[16,128]{1,0:T(8,128)S(1)} %max.16, f32[16,640,128]{2,1,0:T(8,128)} %get-tuple-element.48, ...), kind=kOutput, calls=%fused_computation.11 | convolution fusion | flops 344719360 | bytes 11035264 | tf_op jit(solution)/shard_map/thd,khd->htk/dot_general | solution.py:118
  295.9 3.2 multiply_bitcast_fusion
  299.1 6.0 %copy.255 = f32[640,16,128]{0,2,1:T(8,128)} copy(f32[640,16,128]{2,0,1:T(8,128)} %multiply_bitcast_fusion) | data formatting | bytes 10485760 | tf_op jit(solution)/shard_map/mul | solution.py:131
  305.2 4.1 fusion.25
  313.9 5.4 %copy.257 = f32[2,256,2048]{2,1,0:T(8,128)} copy(f32[2,256,2048]{1,2,0:T(8,128)} %fusion.2) | data formatting | bytes 8388608 | tf_op jit(solution)/shard_map/slice | solution.py:149
  319.4 5.4 %copy.258 = f32[2,2,128,2048]{2,3,0,1:T(8,128)} copy(f32[2,2,128,2048]{3,2,1,0:T(8,128)} %bitcast.147) | data formatting | bytes 8388608 | tf_op jit(solution)/shard_map/reshape | solution.py:149
  324.8 4.8 %fusion = bf16[2,640,2048]{1,2,0:T(8,128)(2,1)S(1)} fusion(f32[1,640,2048]{1,2,0:T(8,128)} %bitcast.142, f32[1,640,2048]{1,2,0:T(8,128)} %bitcast.138), kind=kLoop, calls=%fused_computation.9 | loop fusion | flops 2621440 | bytes 15728640 | tf_op jit(solution)/shard_map/convert.9
  332.5 4.0 collective-permute-start.17
  336.6 2.8 fusion.22
  341.4 14.4 %all-to-all-done.1 = bf16[16,3,2,128,128]{4,3,2,1,0:T(8,128)(2,1)} async-done(((bf16[16,3,2,128,128]{4,3,2,1,0:T(8,128)(2,1)}), bf16[16,3,2,128,128]{4,3,2,1,0:T(8,128)(2,1)}, u32[]{:S(2)}, u32[]{:S(2)}) %all-to-all-start.1) | async-done | bytes 3145760 | tf_op jit(solution)/shard_map/all_to_all | solution.py:170
  355.7 5.0 %fusion.15 = f32[2,128,16,128]{3,2,1,0:T(8,128)} fusion(bf16[16,3,2,128,128]{4,3,2,1,0:T(8,128)(2,1)} %all-to-all-done.1, s32[16,3]{0,1:T(4,128)S(1)} %copy.263), kind=kOutput, calls=%fused_computation.37 | convolution fusion | flops 50332416 | bytes 5243072 | tf_op jit(solution)/shard_map/nmh,nmcbd->cbhd/dot_general | solution.py:174
  362.8 101.7 %all-reduce.4.cloned.1.call-done = f32[2,2,128,2048]{2,3,1,0:T(8,128)} async-done(((f32[2,2,128,2048]{2,3,1,0:T(8,128)}), f32[2,2,128,2048]{2,3,1,0:T(8,128)}) %all-reduce.4.cloned.1.call-update) | async-done | bytes 4194320 | tf_op jit(solution)/shard_map/psum | solution.py:151
  464.5 3.2 fusion.14
  (149 shorter events, 56.9 us)
Async XLA Ops:
  7.2 11.0 %copy-start.11 = (bf16[128,2048]{1,0:T(8,128)(2,1)S(1)}, bf16[128,2048]{1,0:T(8,128)(2,1)}, u32[]{:S(2)}) copy-start(bf16[128,2048]{1,0:T(8,128)(2,1)} %param.6) | copy-start | bytes 1572868
  11.6 7.4 %collective-permute-start.2 = (s32[1,3]{0,1:T(4,128)S(1)}, s32[1,3]{0,1:T(4,128)S(1)}, u32[]{:S(2)}, u32[]{:S(2)}) collective-permute-start(s32[1,3]{0,1:T(4,128)S(1)} %get-tuple-element.45), channel_id=1, source_target_pairs={{0,1},{1,0},{2,3},{3,2},{4,5},{5,4},{6,7},{7,6},{8,9},{9,8},{10,11... | collective-permute-start | bytes 44 | tf_op jit(solution)/shard_map/ppermute | solution.py:22
  12.1 9.7 %collective-permute-start.3 = (s32[1,3]{0,1:T(4,128)S(1)}, s32[1,3]{0,1:T(4,128)S(1)}, u32[]{:S(2)}, u32[]{:S(2)}) collective-permute-start(s32[1,3]{0,1:T(4,128)S(1)} %get-tuple-element.44), channel_id=1, source_target_pairs={{0,2},{1,3},{2,0},{3,1},{4,6},{5,7},{6,4},{7,5},{8,10},{9,11},{10,... | collective-permute-start | bytes 44 | tf_op jit(solution)/shard_map/ppermute | solution.py:22
  14.7 7.4 %collective-permute-start.4 = (s32[1,3]{0,1:T(4,128)S(1)}, s32[1,3]{0,1:T(4,128)S(1)}, u32[]{:S(2)}, u32[]{:S(2)}) collective-permute-start(s32[1,3]{0,1:T(4,128)S(1)} %get-tuple-element.43), channel_id=1, source_target_pairs={{0,3},{1,2},{2,1},{3,0},{4,7},{5,6},{6,5},{7,4},{8,11},{9,10},{10,... | collective-permute-start | bytes 44 | tf_op jit(solution)/shard_map/ppermute | solution.py:22
  14.8 10.2 %collective-permute-start.5 = (s32[1,3]{0,1:T(4,128)S(1)}, s32[1,3]{0,1:T(4,128)S(1)}, u32[]{:S(2)}, u32[]{:S(2)}) collective-permute-start(s32[1,3]{0,1:T(4,128)S(1)} %get-tuple-element.42), channel_id=1, source_target_pairs={{0,4},{1,5},{2,6},{3,7},{4,0},{5,1},{6,2},{7,3},{8,12},{9,13},{10,... | collective-permute-start | bytes 44 | tf_op jit(solution)/shard_map/ppermute | solution.py:22
  16.6 8.6 %collective-permute-start.6 = (s32[1,3]{0,1:T(4,128)S(1)}, s32[1,3]{0,1:T(4,128)S(1)}, u32[]{:S(2)}, u32[]{:S(2)}) collective-permute-start(s32[1,3]{0,1:T(4,128)S(1)} %get-tuple-element.41), channel_id=1, source_target_pairs={{0,5},{1,4},{2,7},{3,6},{4,1},{5,0},{6,3},{7,2},{8,13},{9,12},{10,... | collective-permute-start | bytes 44 | tf_op jit(solution)/shard_map/ppermute | solution.py:22
  19.0 9.9 %collective-permute-start.7 = (s32[1,3]{0,1:T(4,128)S(1)}, s32[1,3]{0,1:T(4,128)S(1)}, u32[]{:S(2)}, u32[]{:S(2)}) collective-permute-start(s32[1,3]{0,1:T(4,128)S(1)} %get-tuple-element.40), channel_id=1, source_target_pairs={{0,6},{1,7},{2,4},{3,5},{4,2},{5,3},{6,0},{7,1},{8,14},{9,15},{10,... | collective-permute-start | bytes 44 | tf_op jit(solution)/shard_map/ppermute | solution.py:22
  21.8 7.3 %collective-permute-start.8 = (s32[1,3]{0,1:T(4,128)S(1)}, s32[1,3]{0,1:T(4,128)S(1)}, u32[]{:S(2)}, u32[]{:S(2)}) collective-permute-start(s32[1,3]{0,1:T(4,128)S(1)} %get-tuple-element.39), channel_id=1, source_target_pairs={{0,7},{1,6},{2,5},{3,4},{4,3},{5,2},{6,1},{7,0},{8,15},{9,14},{10,... | collective-permute-start | bytes 44 | tf_op jit(solution)/shard_map/ppermute | solution.py:22
  22.1 10.8 %collective-permute-start.9 = (s32[1,3]{0,1:T(4,128)S(1)}, s32[1,3]{0,1:T(4,128)S(1)}, u32[]{:S(2)}, u32[]{:S(2)}) collective-permute-start(s32[1,3]{0,1:T(4,128)S(1)} %get-tuple-element.38), channel_id=1, source_target_pairs={{0,8},{1,9},{2,10},{3,11},{4,12},{5,13},{6,14},{7,15},{8,0},{9,1},... | collective-permute-start | bytes 44 | tf_op jit(solution)/shard_map/ppermute | solution.py:22
  24.9 8.1 %collective-permute-start.10 = (s32[1,3]{0,1:T(4,128)S(1)}, s32[1,3]{0,1:T(4,128)S(1)}, u32[]{:S(2)}, u32[]{:S(2)}) collective-permute-start(s32[1,3]{0,1:T(4,128)S(1)} %get-tuple-element.37), channel_id=1, source_target_pairs={{0,9},{1,8},{2,11},{3,10},{4,13},{5,12},{6,15},{7,14},{8,1},{9,0},... | collective-permute-start | bytes 44 | tf_op jit(solution)/shard_map/ppermute | solution.py:22
  25.1 12.6 %collective-permute-start.11 = (s32[1,3]{0,1:T(4,128)S(1)}, s32[1,3]{0,1:T(4,128)S(1)}, u32[]{:S(2)}, u32[]{:S(2)}) collective-permute-start(s32[1,3]{0,1:T(4,128)S(1)} %get-tuple-element.36), channel_id=1, source_target_pairs={{0,10},{1,11},{2,8},{3,9},{4,14},{5,15},{6,12},{7,13},{8,2},{9,3},... | collective-permute-start | bytes 44 | tf_op jit(solution)/shard_map/ppermute | solution.py:22
  28.9 9.1 %collective-permute-start.12 = (s32[1,3]{0,1:T(4,128)S(1)}, s32[1,3]{0,1:T(4,128)S(1)}, u32[]{:S(2)}, u32[]{:S(2)}) collective-permute-start(s32[1,3]{0,1:T(4,128)S(1)} %get-tuple-element.35), channel_id=1, source_target_pairs={{0,11},{1,10},{2,9},{3,8},{4,15},{5,14},{6,13},{7,12},{8,3},{9,2},... | collective-permute-start | bytes 44 | tf_op jit(solution)/shard_map/ppermute | solution.py:22
  29.1 9.0 %collective-permute-start.13 = (s32[1,3]{0,1:T(4,128)S(1)}, s32[1,3]{0,1:T(4,128)S(1)}, u32[]{:S(2)}, u32[]{:S(2)}) collective-permute-start(s32[1,3]{0,1:T(4,128)S(1)} %get-tuple-element.34), channel_id=1, source_target_pairs={{0,12},{1,13},{2,14},{3,15},{4,8},{5,9},{6,10},{7,11},{8,4},{9,5},... | collective-permute-start | bytes 44 | tf_op jit(solution)/shard_map/ppermute | solution.py:22
  32.9 5.3 %collective-permute-start.14 = (s32[1,3]{0,1:T(4,128)S(1)}, s32[1,3]{0,1:T(4,128)S(1)}, u32[]{:S(2)}, u32[]{:S(2)}) collective-permute-start(s32[1,3]{0,1:T(4,128)S(1)} %get-tuple-element.33), channel_id=1, source_target_pairs={{0,13},{1,12},{2,15},{3,14},{4,9},{5,8},{6,11},{7,10},{8,5},{9,4},... | collective-permute-start | bytes 44 | tf_op jit(solution)/shard_map/ppermute | solution.py:22
  33.1 6.3 %collective-permute-start.15 = (s32[1,3]{0,1:T(4,128)S(1)}, s32[1,3]{0,1:T(4,128)S(1)}, u32[]{:S(2)}, u32[]{:S(2)}) collective-permute-start(s32[1,3]{0,1:T(4,128)S(1)} %get-tuple-element.32), channel_id=1, source_target_pairs={{0,14},{1,15},{2,12},{3,13},{4,10},{5,11},{6,8},{7,9},{8,6},{9,7},... | collective-permute-start | bytes 44 | tf_op jit(solution)/shard_map/ppermute | solution.py:22
  37.7 5.8 %collective-permute-start.16 = (s32[1,3]{0,1:T(4,128)S(1)}, s32[1,3]{0,1:T(4,128)S(1)}, u32[]{:S(2)}, u32[]{:S(2)}) collective-permute-start(s32[1,3]{0,1:T(4,128)S(1)} %get-tuple-element.31), channel_id=1, source_target_pairs={{0,15},{1,14},{2,13},{3,12},{4,11},{5,10},{6,9},{7,8},{8,7},{9,6},... | collective-permute-start | bytes 44 | tf_op jit(solution)/shard_map/ppermute | solution.py:22
  50.2 200.8 %all-to-all-start = ((bf16[16,3,2,128,128]{4,3,2,1,0:T(8,128)(2,1)}), bf16[16,3,2,128,128]{4,3,2,1,0:T(8,128)(2,1)}, u32[]{:S(2)}, u32[]{:S(2)}) async-start(bf16[16,3,2,128,128]{4,3,2,1,0:T(8,128)(2,1)} %broadcast_select_fusion), calls=%async_computation | async-start | bytes 6291456 | tf_op jit(solution)/shard_map/all_to_all | solution.py:71
  54.7 183.3 %all-reduce.6.cloned.1.call-start = ((), (), s32[]{:S(2)}) async-start(), calls=%async_computation.3 | async-start | bytes 4194304 | tf_op jit(solution)/shard_map/psum | solution.py:42
  54.8 4.4 collective-permute-start
  57.0 9.2 %collective-permute-start.1 = (bf16[2,128,2048]{1,2,0:T(8,128)(2,1)S(1)}, bf16[2,128,2048]{1,2,0:T(8,128)(2,1)}, u32[]{:S(2)}, u32[]{:S(2)}) collective-permute-start(bf16[2,128,2048]{1,2,0:T(8,128)(2,1)S(1)} %pad_maximum_fusion.5), channel_id=1, source_target_pairs={{1,0},{2,1},{3,2},{4,3},{5,4},{6,5},{7,6},{8,7},{9,8},{10,9},{11,1... | collective-permute-start | bytes 3145736 | tf_op jit(solution)/shard_map/ppermute | solution.py:35
  59.4 4.4 copy-start.12
  242.7 4.6 copy-start.8
  257.7 9.9 %copy-start.3 = (bf16[48,2,128,128]{3,2,0,1:T(8,128)(2,1)}, bf16[48,2,128,128]{3,2,0,1:T(8,128)(2,1)S(1)}, u32[]{:S(2)}) copy-start(bf16[48,2,128,128]{3,2,0,1:T(8,128)(2,1)S(1)} %copy.240) | copy-start | bytes 9437188
  257.8 3.6 copy-start.2
  284.1 71.6 %all-to-all-start.1 = ((bf16[16,3,2,128,128]{4,3,2,1,0:T(8,128)(2,1)}), bf16[16,3,2,128,128]{4,3,2,1,0:T(8,128)(2,1)}, u32[]{:S(2)}, u32[]{:S(2)}) async-start(bf16[16,3,2,128,128]{4,3,2,1,0:T(8,128)(2,1)} %scatter_fusion.1), calls=%async_computation.1 | async-start | bytes 6291456 | tf_op jit(solution)/shard_map/all_to_all | solution.py:170
  288.6 7.3 %copy-start.9 = (bf16[128,16,128]{0,2,1:T(8,128)(2,1)S(1)}, bf16[128,16,128]{0,2,1:T(8,128)(2,1)}, u32[]{:S(2)}) copy-start(bf16[128,16,128]{0,2,1:T(8,128)(2,1)} %copy.253) | copy-start | bytes 1572868
  288.6 175.9 %all-reduce.4.cloned.1.call-start = ((), (), s32[]{:S(2)}) async-start(), calls=%async_computation.2 | async-start | bytes 8388608 | tf_op jit(solution)/shard_map/psum | solution.py:151
  299.1 6.0 %copy-start.15 = (bf16[128,2048]{0,1:T(8,128)(2,1)S(1)}, bf16[128,2048]{0,1:T(8,128)(2,1)}, u32[]{:S(2)}) copy-start(bf16[128,2048]{0,1:T(8,128)(2,1)} %copy.242) | copy-start | bytes 1572868
  305.2 6.5 %copy-start = (f32[640,16,128]{0,2,1:T(8,128)S(1)}, f32[640,16,128]{0,2,1:T(8,128)}, u32[]{:S(2)}) copy-start(f32[640,16,128]{0,2,1:T(8,128)} %copy.255) | copy-start | bytes 15728644
  331.2 31.5 %collective-permute-start.18 = (bf16[2,128,2048]{1,2,0:T(8,128)(2,1)}, bf16[2,128,2048]{1,2,0:T(8,128)(2,1)}, u32[]{:S(2)}, u32[]{:S(2)}) collective-permute-start(bf16[2,128,2048]{1,2,0:T(8,128)(2,1)} %get-tuple-element.23), channel_id=1, source_target_pairs={{1,0},{2,1},{3,2},{4,3},{5,4},{6,5},{7,6},{8,7},{9,8},{10,9},{11,1... | collective-permute-start | bytes 3145736 | tf_op jit(solution)/shard_map/ppermute | solution.py:35
  332.5 30.3 %collective-permute-start.17 = (bf16[2,128,2048]{1,2,0:T(8,128)(2,1)}, bf16[2,128,2048]{1,2,0:T(8,128)(2,1)}, u32[]{:S(2)}, u32[]{:S(2)}) collective-permute-start(bf16[2,128,2048]{1,2,0:T(8,128)(2,1)} %get-tuple-element.22), channel_id=1, source_target_pairs={{0,1},{1,2},{2,3},{3,4},{4,5},{5,6},{6,7},{7,8},{8,9},{9,10},{10,1... | collective-permute-start | bytes 3145736 | tf_op jit(solution)/shard_map/ppermute | solution.py:34
  336.6 2.8 copy-start.5
  (7 other events, 11.3 us)
Sparse Core Ops, SparseCore 0:
  63.9 173.9 all-reduce.5
  324.9 139.6 all-reduce.3
